TPU v7x, 32 devices: a whole 2x2x4 slice. The times are simulated.
32 devices in a mesh: row: 4 (over y, x), col: 4 (over z), depth: 2 (over core).
Axes of the slice: x: 2, y: 2, z: 4, core: 2. Of those that a mesh axis runs over, the one named last changes fastest.
Arguments:
- a_blocks: bfloat16 [32, 32, 2, 128, 128], P(('row', 'col', 'depth')), may hold values from -1.25 to 1.25
- a_columns: int32 [32, 32, 2], P(('row', 'col', 'depth')), may hold values from 0 to 319, as said below
- a_live: int32 [32, 32, 2], P(('row', 'col', 'depth')), may hold values from 0 to 1
- atom_rows: int32 [32], P(('row', 'col', 'depth')), may hold values from 0 to 31, as said below
- b_blocks: bfloat16 [320, 4, 6, 128, 128], P(('row', 'depth'), 'col'), may hold values from -1.25 to 1.25
- b_columns: int32 [320, 4, 6], P(('row', 'depth'), 'col'), may hold values from 0 to 319, as said below
- b_live: int32 [320, 4, 6], P(('row', 'depth'), 'col'), may hold values from 0 to 1, as said below
- c_columns: int32 [32, 4, 8], P('row', 'col'), may hold values from 0 to 319, as said below
- c_live: int32 [32, 4, 8], P('row', 'col'), may hold values from 0 to 1
Outputs:
- product: bfloat16 [32, 4, 8, 128, 128], P('row', 'col', 'depth')
Inputs may be any that keep to these rules, and one draw needn't show every extreme that they name: `a_columns`: columns of one block row and group g are distinct and lie in g * 10 to (g + 1) * 10 - 1, also in empty slots. `atom_rows`: A permutation that maps every aligned run of 8 atom-order rows onto the same run of block rows. `b_columns`: columns of one block row and panel c are distinct and lie in c * 80 to (c + 1) * 80 - 1, also in empty slots. `b_live`: live slots of block row k hold columns within 16 of k, counted round. `c_columns`: columns of one block row and panel c are distinct and lie in c * 80 to (c + 1) * 80 - 1.
All inputs are finite; a program needn't handle non-finite values.
Results may differ from a plain program's by a relative error of at most 0.0043.
Values may be sent and summed in bfloat16 or wider, within the bound.
A program may use at most 320 MiB of HBM per device.

v0:
```python
import jax
import jax.numpy as jnp
from jax import lax
from jax.sharding import PartitionSpec as P

GW = 10


def shifted(value, axis, by):
    length = lax.axis_size(axis)
    return lax.ppermute(value, axis, [(i, (i + by) % length) for i in range(length)])


def on_device(
    a_blocks, a_columns, a_live, atom_rows, b_blocks, b_columns, b_live, c_columns, c_live
):
    row_count = lax.axis_size("row")
    col_count = lax.axis_size("col")
    depth_count = lax.axis_size("depth")
    turn_count = min(row_count, col_count)
    row_index = lax.axis_index("row")
    own_rows, group_count, slot_count = a_columns.shape
    block_edge = a_blocks.shape[-1]
    stripe = b_blocks.shape[0]
    per_stripe = stripe // GW
    stripes_piece = row_count // turn_count
    piece_groups = stripes_piece * per_stripe
    dest_col = jnp.arange(col_count, dtype=jnp.int32)[:, None, None]
    dest_layer = jnp.arange(depth_count, dtype=jnp.int32)[None, :, None]
    within = jnp.arange(piece_groups, dtype=jnp.int32)[None, None, :]
    piece_of = (dest_col + row_index) % turn_count
    stripe_ids = (piece_of * stripes_piece + within // per_stripe) * depth_count + dest_layer
    group_ids = (stripe_ids * per_stripe + within % per_stripe).reshape(-1)
    lead_shape = (col_count, depth_count, own_rows, piece_groups, slot_count)
    send_blocks = jnp.moveaxis(jnp.take(a_blocks, group_ids, axis=1), 1, 0).reshape(
        lead_shape + (block_edge, block_edge)
    )
    send_columns = jnp.moveaxis(jnp.take(a_columns, group_ids, axis=1), 1, 0).reshape(lead_shape)
    outgoing_live_flags = jnp.moveaxis(jnp.take(a_live, group_ids, axis=1), 1, 0).reshape(
        lead_shape
    )
    send_rows = jnp.broadcast_to(atom_rows[None, None, :], (col_count, depth_count, own_rows))
    pair_count = col_count * depth_count
    got_blocks, got_columns, got_live, got_rows = (
        lax.all_to_all(
            send_blocks.reshape((pair_count,) + lead_shape[2:] + (block_edge, block_edge)),
            ("col", "depth"),
            split_axis=0,
            concat_axis=0,
            tiled=True,
        ),
        lax.all_to_all(
            send_columns.reshape((pair_count,) + lead_shape[2:]),
            ("col", "depth"),
            split_axis=0,
            concat_axis=0,
            tiled=True,
        ),
        lax.all_to_all(
            outgoing_live_flags.reshape((pair_count,) + lead_shape[2:]),
            ("col", "depth"),
            split_axis=0,
            concat_axis=0,
            tiled=True,
        ),
        lax.all_to_all(
            send_rows.reshape(pair_count, own_rows),
            ("col", "depth"),
            split_axis=0,
            concat_axis=0,
            tiled=True,
        ),
    )
    panel_rows = got_rows.reshape(-1)
    panel_count = panel_rows.shape[0]
    local_rows = panel_rows - row_index * panel_count
    positions = jnp.arange(panel_count, dtype=jnp.int32)
    matched_pairs = local_rows[None, :] == positions[:, None]
    source_of = jnp.sum(jnp.where(matched_pairs, positions[None, :], 0), axis=1)
    block_tiles = got_blocks.reshape(panel_count, -1, block_edge, block_edge)
    columns = got_columns.reshape(panel_count, -1)
    live_flags = got_live.reshape(panel_count, -1)
    layer_blocks, layer_columns, layer_active_flags = (
        lax.all_gather(b_blocks, "row", axis=0, tiled=True),
        lax.all_gather(b_columns, "row", axis=0, tiled=True),
        lax.all_gather(b_live, "row", axis=0, tiled=True),
    )
    list_width = b_columns.shape[2]
    layer_blocks = layer_blocks.reshape(-1, list_width, block_edge, block_edge)
    layer_columns = layer_columns.reshape(-1, list_width)
    layer_active_flags = layer_active_flags.reshape(-1, list_width)
    wanted = jnp.take(c_columns[:, 0, :], local_rows, axis=0)
    partial_value = jnp.zeros((panel_count, wanted.shape[1], block_edge, block_edge), jnp.float32)
    for turn_index in range(turn_count):
        layer_row_index = columns // stripe // depth_count * stripe + columns % stripe
        found_columns = jnp.take(layer_columns, layer_row_index, axis=0)
        found_live = jnp.take(layer_active_flags, layer_row_index, axis=0)
        usable = (found_live > 0) & (live_flags[:, :, None] > 0)
        hits = (found_columns[:, None, :, :] == wanted[:, :, None, None]) & usable[:, None, :, :]
        mapping = hits.astype(jnp.float32)
        selected_entries = jnp.take(layer_blocks, layer_row_index, axis=0)
        block_products = jnp.einsum(
            "rvab,rvsbe->rvsae", block_tiles, selected_entries, preferred_element_type=jnp.float32
        )
        partial_value = partial_value + jnp.einsum(
            "ruvs,rvsae->ruae", mapping, block_products, precision=lax.Precision.HIGHEST
        )
        if turn_index + 1 < turn_count:
            block_tiles, columns, live_flags = shifted(
                (block_tiles, columns, live_flags), "col", -1
            )
    share_count = wanted.shape[1] // depth_count
    depth_index = lax.axis_index("depth")
    summed = lax.psum(partial_value.astype(jnp.bfloat16), "depth").astype(jnp.float32)
    my_share = lax.dynamic_slice_in_dim(summed, depth_index * share_count, share_count, 1)
    my_share = jnp.take(my_share, source_of, axis=0)
    keep_flags = lax.dynamic_slice_in_dim(
        c_live[:, 0, :], depth_index * share_count, share_count, 1
    )
    result = jnp.where(keep_flags[..., None, None] > 0, my_share, jnp.float32(0.0)).astype(
        jnp.bfloat16
    )
    return result[:, None]


def solution(mesh):
    placed = (
        P(("row", "col", "depth"), None, None, None, None),
        P(("row", "col", "depth"), None, None),
        P(("row", "col", "depth"), None, None),
        P(("row", "col", "depth")),
        P(("row", "depth"), "col", None, None, None),
        P(("row", "depth"), "col", None),
        P(("row", "depth"), "col", None),
        P("row", "col", None),
        P("row", "col", None),
    )
    return jax.shard_map(
        on_device,
        mesh=mesh,
        in_specs=placed,
        out_specs=P("row", "col", "depth", None, None),
        check_vma=False,
    )
```

profile of v0, /device:TPU:0, one launch (start us, length us, event | category | flops | bytes accessed | tf_op | source)
XLA Modules:
  0.0 684.4 jit_solution(8725497915445718610)
XLA Ops:
  8.5 6.3 all-to-all-start
  17.2 4.0 broadcast_select_fusion
  21.2 5.2 all-to-all-start.3
  29.6 9.1 %all_gather.10 = s32[160,1,6]{2,0,1:T(8,128)S(1)} all-gather(s32[40,1,6]{2,0,1:T(8,128)S(1)} %copy.229), channel_id=1, replica_groups=mesh['row'=4,'col'=4,'depth'=2] {'row'}, dimensions={0}, use_global_device_ids=true | all-gather | bytes 4800 | tf_op jit(solution)/shard_map/all_gather | solution.py:86
  38.6 9.1 %all_gather.9 = s32[160,1,6]{2,0,1:T(8,128)S(1)} all-gather(s32[40,1,6]{2,0,1:T(8,128)S(1)} %copy.225), channel_id=1, replica_groups=mesh['row'=4,'col'=4,'depth'=2] {'row'}, dimensions={0}, use_global_device_ids=true | all-gather | bytes 4800 | tf_op jit(solution)/shard_map/all_gather | solution.py:85
  48.0 27.6 %all-to-all-done.3 = bf16[8,1,4,2,128,128]{5,4,3,2,1,0:T(8,128)(2,1)} async-done(((bf16[8,1,4,2,128,128]{5,4,3,2,1,0:T(8,128)(2,1)}), bf16[8,1,4,2,128,128]{5,4,3,2,1,0:T(8,128)(2,1)}, u32[]{:S(2)}, u32[]{:S(2)}) %all-to-all-start.3) | async-done | bytes 2097184 | tf_op jit(solution)/shard_map/all_to_all | solution.py:45
  78.9 3.8 collective-permute-start.2
  88.0 3.8 collective-permute-start
  92.0 37.3 %all-to-all-done.2 = s32[8,1,4,2]{2,3,1,0:T(2,128)S(1)} async-done(((s32[8,1,4,2]{2,3,1,0:T(2,128)}), s32[8,1,4,2]{2,3,1,0:T(2,128)S(1)}, u32[]{:S(2)}, u32[]{:S(2)}) %all-to-all-start.2) | async-done | bytes 288 | tf_op jit(solution)/shard_map/all_to_all | solution.py:59
  142.2 42.9 %collective-permute-done.4 = s32[8,8]{0,1:T(8,128)S(1)} collective-permute-done((s32[8,8]{0,1:T(8,128)S(1)}, s32[8,8]{0,1:T(8,128)S(1)}, u32[]{:S(2)}, u32[]{:S(2)}) %collective-permute-start.4) | collective-permute-done | bytes 288 | tf_op jit(solution)/shard_map/ppermute | solution.py:11
  197.2 95.8 %all-gather.2.cloned.1.call-done = bf16[160,1,6,128,128]{4,3,2,1,0:T(8,128)(2,1)} async-done(((bf16[40,1,6,128,128]{4,3,2,1,0:T(8,128)(2,1)}), bf16[160,1,6,128,128]{4,3,2,1,0:T(8,128)(2,1)}) %all-gather.2.cloned.1.call-update) | async-done | bytes 31457296 | tf_op jit(solution)/shard_map/all_gather | solution.py:84
  293.0 17.2 %gather_fusion.7 = bf16[64,6,128,128]{3,2,1,0:T(8,128)(2,1)} fusion(bf16[160,6,128,128]{3,2,1,0:T(8,128)(2,1)} %bitcast.147, s32[1024]{0:T(1024)S(1)} %pad_clamp_fusion.6), kind=kCustom, calls=%fused_computation.2.clone | custom fusion | bytes 25166080 | tf_op jit(solution)/shard_map/jit(_take)/gather | solution.py:101
  310.3 17.2 %gather_fusion.10 = bf16[64,6,128,128]{3,2,1,0:T(8,128)(2,1)} fusion(bf16[160,6,128,128]{3,2,1,0:T(8,128)(2,1)} %bitcast.148, s32[1024]{0:T(1024)S(1)} %pad_clamp_fusion.3), kind=kCustom, calls=%fused_computation.11.clone | custom fusion | bytes 25166080 | tf_op jit(solution)/shard_map/jit(_take)/gather | solution.py:101
  327.5 16.6 %copy.239 = bf16[8,8,6,128,128]{3,4,2,1,0:T(8,128)(2,1)} copy(bf16[8,8,6,128,128]{4,3,2,1,0:T(8,128)(2,1)} %bitcast.153) | data formatting | bytes 25165824 | tf_op jit(solution)/shard_map/jit(_take)/gather | solution.py:101
  344.1 16.7 %copy.250 = bf16[8,8,6,128,128]{3,4,2,1,0:T(8,128)(2,1)} copy(bf16[8,8,6,128,128]{4,3,2,1,0:T(8,128)(2,1)} %bitcast.154) | data formatting | bytes 25165824 | tf_op jit(solution)/shard_map/jit(_take)/gather | solution.py:101
  360.8 13.6 %fusion.12 = f32[8,8,6,128,128]{3,4,2,1,0:T(8,128)} fusion(bf16[8,8,128,128,1]{3,2,4,1,0:T(8,128)(2,1)} %bitcast.24, bf16[8,8,6,128,128]{3,4,2,1,0:T(8,128)(2,1)} %copy.239, pred[8,8]{1,0:T(8,128)(4,1)S(1)} %copy.224), kind=kOutput, calls=%fused_computation.29 | convolution fusion | flops 1616904192 | bytes 39845952 | tf_op jit(solution)/shard_map/rvab,rvsbe->rvsae/dot_general | solution.py:102
  374.4 13.7 %fusion.15 = f32[8,8,6,128,128]{3,4,2,1,0:T(8,128)} fusion(bf16[8,8,6,128,128]{3,4,2,1,0:T(8,128)(2,1)} %copy.250, pred[8,8]{1,0:T(8,128)(4,1)S(1)} %copy.241, bf16[8,8,128,128]{3,2,1,0:T(8,128)(2,1)} %collective-permute-done.2), kind=kOutput, calls=%fused_computation.30 | convolution fusion | flops 1616904192 | bytes 39845952 | tf_op jit(solution)/shard_map/rvab,rvsbe->rvsae/dot_general | solution.py:102
  388.1 17.3 %gather_fusion.13 = bf16[64,6,128,128]{3,2,1,0:T(8,128)(2,1)} fusion(bf16[160,6,128,128]{3,2,1,0:T(8,128)(2,1)} %bitcast.149, s32[1024]{0:T(1024)S(1)} %pad_clamp_fusion.2), kind=kCustom, calls=%fused_computation.12.clone | custom fusion | bytes 25166080 | tf_op jit(solution)/shard_map/jit(_take)/gather | solution.py:101
  405.4 17.2 %gather_fusion.16 = bf16[64,6,128,128]{3,2,1,0:T(8,128)(2,1)} fusion(bf16[160,6,128,128]{3,2,1,0:T(8,128)(2,1)} %bitcast.150, s32[1024]{0:T(1024)S(1)} %pad_clamp_fusion.1), kind=kCustom, calls=%fused_computation.13.clone | custom fusion | bytes 25166080 | tf_op jit(solution)/shard_map/jit(_take)/gather | solution.py:101
  422.5 24.8 %copy.240 = f32[8,8,6,128,128]{4,1,2,3,0:T(8,128)} copy(f32[8,8,6,128,128]{3,4,2,1,0:T(8,128)} %fusion.12) | data formatting | bytes 50331648 | tf_op jit(solution)/shard_map/rvab,rvsbe->rvsae/transpose | solution.py:102
  447.3 24.9 %copy.251 = f32[8,8,6,128,128]{4,1,2,3,0:T(8,128)} copy(f32[8,8,6,128,128]{3,4,2,1,0:T(8,128)} %fusion.15) | data formatting | bytes 50331648 | tf_op jit(solution)/shard_map/rvab,rvsbe->rvsae/transpose | solution.py:102
  472.2 16.6 %copy.272 = bf16[8,8,6,128,128]{3,4,2,1,0:T(8,128)(2,1)} copy(bf16[8,8,6,128,128]{4,3,2,1,0:T(8,128)(2,1)} %bitcast.152) | data formatting | bytes 25165824 | tf_op jit(solution)/shard_map/jit(_take)/gather | solution.py:101
  488.8 16.7 %copy.261 = bf16[8,8,6,128,128]{3,4,2,1,0:T(8,128)(2,1)} copy(bf16[8,8,6,128,128]{4,3,2,1,0:T(8,128)(2,1)} %bitcast.151) | data formatting | bytes 25165824 | tf_op jit(solution)/shard_map/jit(_take)/gather | solution.py:101
  505.5 13.8 %fusion.18 = f32[8,8,6,128,128]{3,4,2,1,0:T(8,128)} fusion(bf16[8,8,6,128,128]{3,4,2,1,0:T(8,128)(2,1)} %copy.261, pred[8,8]{1,0:T(8,128)(4,1)S(1)} %copy.252, bf16[8,8,128,128]{3,2,1,0:T(8,128)(2,1)} %collective-permute-done.5), kind=kOutput, calls=%fused_computation.31 | convolution fusion | flops 1616904192 | bytes 39845952 | tf_op jit(solution)/shard_map/rvab,rvsbe->rvsae/dot_general | solution.py:102
  519.2 24.8 %copy.262 = f32[8,8,6,128,128]{4,1,2,3,0:T(8,128)} copy(f32[8,8,6,128,128]{3,4,2,1,0:T(8,128)} %fusion.18) | data formatting | bytes 50331648 | tf_op jit(solution)/shard_map/rvab,rvsbe->rvsae/transpose | solution.py:102
  544.0 12.9 %fusion.21 = f32[8,8,6,128,128]{3,4,2,1,0:T(8,128)} fusion(bf16[8,8,6,128,128]{3,4,2,1,0:T(8,128)(2,1)} %copy.272, pred[8,8]{1,0:T(8,128)(4,1)S(1)} %copy.263, bf16[8,8,128,128]{3,2,1,0:T(8,128)(2,1)S(1)} %collective-permute-done.8), kind=kOutput, calls=%fused_computation.32 | convolution fusion | flops 1616904192 | bytes 39845952 | tf_op jit(solution)/shard_map/rvab,rvsbe->rvsae/dot_general | solution.py:102
  556.9 24.9 %copy.273 = f32[8,8,6,128,128]{4,1,2,3,0:T(8,128)} copy(f32[8,8,6,128,128]{3,4,2,1,0:T(8,128)} %fusion.21) | data formatting | bytes 50331648 | tf_op jit(solution)/shard_map/rvab,rvsbe->rvsae/transpose | solution.py:102
  581.9 15.6 %fusion.39 = f32[8,8,128,128,1]{3,1,4,2,0:T(8,128)} fusion(f32[8,8,6,128,128]{4,1,2,3,0:T(8,128)} %copy.240, s32[8,8]{1,0:T(8,128)S(1)} %copy-done.7, s32[8,8,6]{1,2,0:T(8,128)S(1)} %copy-done.3, pred[8,8,6]{1,2,0:T(8,128)(4,1)S(1)} %copy-done.8), kind=kOutput, calls=%fused_computation.54 | convolution fusion | flops 603985920 | bytes 29362304 | tf_op jit(solution)/shard_map/ruvs,rvsae->ruae/dot_general | solution.py:105
  597.5 15.6 %fusion.37 = f32[8,8,128,128,1]{3,1,4,2,0:T(8,128)} fusion(f32[8,8,6,128,128]{4,1,2,3,0:T(8,128)} %copy.251, s32[8,8,6]{1,2,0:T(8,128)S(1)} %copy-done.4, s32[8,8]{1,0:T(8,128)S(1)} %copy-done.7, pred[8,8,6]{1,2,0:T(8,128)(4,1)S(1)} %copy-done.9), kind=kOutput, calls=%fused_computation.52 | convolution fusion | flops 603985920 | bytes 29362304 | tf_op jit(solution)/shard_map/ruvs,rvsae->ruae/dot_general | solution.py:105
  613.1 15.9 %fusion.35 = f32[8,8,128,128,1]{3,1,4,2,0:T(8,128)} fusion(f32[8,8,6,128,128]{4,1,2,3,0:T(8,128)} %copy.262, s32[8,8,6]{1,2,0:T(8,128)S(1)} %copy-done.5, s32[8,8]{1,0:T(8,128)S(1)} %copy-done.7, pred[8,8,6]{1,2,0:T(8,128)(4,1)S(1)} %copy-done.10), kind=kOutput, calls=%fused_computation.50 | convolution fusion | flops 603985920 | bytes 29362304 | tf_op jit(solution)/shard_map/ruvs,rvsae->ruae/dot_general | solution.py:105
  629.0 19.4 %fusion.28 = bf16[8,8,128,128]{3,1,2,0:T(8,128)(2,1)} fusion(f32[8,8,128,128,1]{3,1,4,2,0:T(8,128)} %fusion.35, f32[8,8,128,128,1]{3,1,4,2,0:T(8,128)} %fusion.37, f32[8,8,128,128,1]{3,1,4,2,0:T(8,128)} %fusion.39, f32[8,8,6,128,128]{4,1,2,3,0:T(8,128)} %copy.273, s32[8,8,6]{1,2,0:T(8,128)S(1)} %copy-done.6, s32[8,8]{1,0:T(8,128)S(1)} %copy-done.7, ...), kind=kOutput, calls=%fused_computation.38 | convolution fusion | flops 608180224 | bytes 39848064 | tf_op jit(solution)/shard_map/ruvs,rvsae->ruae/dot_general | solution.py:105
  648.8 20.9 %all-reduce.2.cloned.1.call-done = bf16[8,8,128,128]{3,1,2,0:T(8,128)(2,1)} async-done(((bf16[8,8,128,128]{3,1,2,0:T(8,128)(2,1)}), bf16[8,8,128,128]{3,1,2,0:T(8,128)(2,1)}) %all-reduce.2.cloned.1.call-update) | async-done | bytes 2097168 | tf_op jit(solution)/shard_map/psum | solution.py:114
  (160 shorter events, 48.9 us)
Async XLA Ops:
  6.5 20.0 %copy-start.15 = (s32[1,32,2]{1,2,0:T(2,128)S(1)}, s32[1,32,2]{1,2,0:T(2,128)}, u32[]{:S(2)}) copy-start(s32[1,32,2]{1,2,0:T(2,128)} %param.16) | copy-start | bytes 772
  6.5 20.7 %copy-start.16 = (s32[1,32,2]{1,2,0:T(2,128)S(1)}, s32[1,32,2]{1,2,0:T(2,128)}, u32[]{:S(2)}) copy-start(s32[1,32,2]{1,2,0:T(2,128)} %param.17) | copy-start | bytes 772
  6.5 22.9 %copy-start.13 = (s32[40,1,6]{0,1,2:T(1,128)S(1)}, s32[40,1,6]{0,1,2:T(1,128)}, u32[]{:S(2)}) copy-start(s32[40,1,6]{0,1,2:T(1,128)} %param.20) | copy-start | bytes 2884
  6.5 22.9 %copy-start.14 = (s32[40,1,6]{0,1,2:T(1,128)S(1)}, s32[40,1,6]{0,1,2:T(1,128)}, u32[]{:S(2)}) copy-start(s32[40,1,6]{0,1,2:T(1,128)} %param.21) | copy-start | bytes 2884
  6.5 76.1 %copy-start.2 = (s32[8,1,8]{2,1,0:T(1,128)S(1)}, s32[8,1,8]{2,1,0:T(1,128)}, u32[]{:S(2)}) copy-start(s32[8,1,8]{2,1,0:T(1,128)} %param.22) | copy-start | bytes 772
  6.6 286.5 %all-gather.2.cloned.1.call-start = ((), (), s32[]{:S(2)}) async-start(), calls=%async_computation.4 | async-start | bytes 39321600 | tf_op jit(solution)/shard_map/all_gather | solution.py:84
  8.5 12.7 %all-to-all-start = ((s32[8,1,1]{2,1,0:T(1,128)}), s32[8,1,1]{2,1,0:T(1,128)S(1)}, u32[]{:S(2)}, u32[]{:S(2)}) async-start(s32[8,1,1]{2,1,0:T(1,128)} %reshape.365), calls=%async_computation | async-start | bytes 8192 | tf_op jit(solution)/shard_map/all_to_all | solution.py:66
  21.2 54.4 %all-to-all-start.3 = ((bf16[8,1,4,2,128,128]{5,4,3,2,1,0:T(8,128)(2,1)}), bf16[8,1,4,2,128,128]{5,4,3,2,1,0:T(8,128)(2,1)}, u32[]{:S(2)}, u32[]{:S(2)}) async-start(bf16[8,1,4,2,128,128]{5,4,3,2,1,0:T(8,128)(2,1)} %broadcast_select_fusion), calls=%async_computation.3 | async-start | bytes 4194304 | tf_op jit(solution)/shard_map/all_to_all | solution.py:45
  47.9 36.6 %copy-start.17 = (s32[8]{0:T(128)}, s32[8]{0:T(128)S(1)}, u32[]{:S(2)}) copy-start(s32[8]{0:T(128)S(1)} %subtract_reduce_fusion) | copy-start | bytes 100
  75.6 8.9 %all-to-all-start.1 = ((s32[8,1,4,2]{2,3,1,0:T(2,128)}), s32[8,1,4,2]{2,3,1,0:T(2,128)S(1)}, u32[]{:S(2)}, u32[]{:S(2)}) async-start(s32[8,1,4,2]{2,3,1,0:T(2,128)} %copy.222), calls=%async_computation.1 | async-start | bytes 16384 | tf_op jit(solution)/shard_map/all_to_all | solution.py:52
  78.9 59.5 %collective-permute-start.2 = (bf16[8,8,128,128]{3,2,1,0:T(8,128)(2,1)}, bf16[8,8,128,128]{3,2,1,0:T(8,128)(2,1)}, u32[]{:S(2)}, u32[]{:S(2)}) collective-permute-start(bf16[8,8,128,128]{3,2,1,0:T(8,128)(2,1)} %bitcast.22), channel_id=1, source_target_pairs={{0,6},{2,0},{4,2},{6,4},{1,7},{3,1},{5,3},{7,5},{8,14},{10,8},{12,... | collective-permute-start | bytes 6291464 | tf_op jit(solution)/shard_map/ppermute | solution.py:11
  84.5 44.8 %all-to-all-start.2 = ((s32[8,1,4,2]{2,3,1,0:T(2,128)}), s32[8,1,4,2]{2,3,1,0:T(2,128)S(1)}, u32[]{:S(2)}, u32[]{:S(2)}) async-start(s32[8,1,4,2]{2,3,1,0:T(2,128)} %copy.233), calls=%async_computation.2 | async-start | bytes 16384 | tf_op jit(solution)/shard_map/all_to_all | solution.py:59
  87.8 582.0 %all-reduce.2.cloned.1.call-start = ((), (), s32[]{:S(2)}) async-start(), calls=%async_computation.5 | async-start | bytes 4194304 | tf_op jit(solution)/shard_map/psum | solution.py:114
  88.0 47.7 %collective-permute-start = (s32[8,8]{0,1:T(8,128)S(1)}, s32[8,8]{0,1:T(8,128)S(1)}, u32[]{:S(2)}, u32[]{:S(2)}) collective-permute-start(s32[8,8]{0,1:T(8,128)S(1)} %bitcast.168), channel_id=1, source_target_pairs={{0,6},{2,0},{4,2},{6,4},{1,7},{3,1},{5,3},{7,5},{8,14},{10,8},{12,... | collective-permute-start | bytes 776 | tf_op jit(solution)/shard_map/ppermute | solution.py:11
  129.4 7.6 %collective-permute-start.1 = (s32[8,8]{0,1:T(8,128)S(1)}, s32[8,8]{0,1:T(8,128)S(1)}, u32[]{:S(2)}, u32[]{:S(2)}) collective-permute-start(s32[8,8]{0,1:T(8,128)S(1)} %bitcast.165), channel_id=1, source_target_pairs={{0,6},{2,0},{4,2},{6,4},{1,7},{3,1},{5,3},{7,5},{8,14},{10,8},{12,... | collective-permute-start | bytes 776 | tf_op jit(solution)/shard_map/ppermute | solution.py:11
  137.2 3.6 collective-permute-start.3
  138.4 56.6 %collective-permute-start.5 = (bf16[8,8,128,128]{3,2,1,0:T(8,128)(2,1)}, bf16[8,8,128,128]{3,2,1,0:T(8,128)(2,1)}, u32[]{:S(2)}, u32[]{:S(2)}) collective-permute-start(bf16[8,8,128,128]{3,2,1,0:T(8,128)(2,1)} %collective-permute-done.2), channel_id=1, source_target_pairs={{0,6},{2,0},{4,2},{6,4},{1,7},{3,1},{5,3},{7,5},{8,14},{10,8},{12,... | collective-permute-start | bytes 6291464 | tf_op jit(solution)/shard_map/ppermute | solution.py:11
  140.0 45.1 %collective-permute-start.4 = (s32[8,8]{0,1:T(8,128)S(1)}, s32[8,8]{0,1:T(8,128)S(1)}, u32[]{:S(2)}, u32[]{:S(2)}) collective-permute-start(s32[8,8]{0,1:T(8,128)S(1)} %collective-permute-done.1), channel_id=1, source_target_pairs={{0,6},{2,0},{4,2},{6,4},{1,7},{3,1},{5,3},{7,5},{8,14},{10,8},{12,... | collective-permute-start | bytes 776 | tf_op jit(solution)/shard_map/ppermute | solution.py:11
  185.3 4.3 collective-permute-start.6
  189.6 3.6 collective-permute-start.7
  195.0 349.1 %collective-permute-start.8 = (bf16[8,8,128,128]{3,2,1,0:T(8,128)(2,1)}, bf16[8,8,128,128]{3,2,1,0:T(8,128)(2,1)S(1)}, u32[]{:S(2)}, u32[]{:S(2)}) collective-permute-start(bf16[8,8,128,128]{3,2,1,0:T(8,128)(2,1)} %collective-permute-done.5), channel_id=1, source_target_pairs={{0,6},{2,0},{4,2},{6,4},{1,7},{3,1},{5,3},{7,5},{8,14},{10,8},{12,... | collective-permute-start | bytes 6291464 | tf_op jit(solution)/shard_map/ppermute | solution.py:11
  556.9 24.9 %copy-start.3 = (s32[8,8,6]{1,2,0:T(8,128)S(1)}, s32[8,8,6]{1,2,0:T(8,128)}, u32[]{:S(2)}) copy-start(s32[8,8,6]{1,2,0:T(8,128)} %copy.227) | copy-start | bytes 4612
  556.9 24.9 %copy-start.7 = (s32[8,8]{1,0:T(8,128)S(1)}, s32[8,8]{1,0:T(8,128)}, u32[]{:S(2)}) copy-start(s32[8,8]{1,0:T(8,128)} %broadcast_select_fusion.1) | copy-start | bytes 772
  556.9 24.9 %copy-start.8 = (pred[8,8,6]{1,2,0:T(8,128)(4,1)S(1)}, pred[8,8,6]{1,2,0:T(8,128)(4,1)}, u32[]{:S(2)}) copy-start(pred[8,8,6]{1,2,0:T(8,128)(4,1)} %copy.236) | copy-start | bytes 1156
  581.8 15.7 %copy-start.4 = (s32[8,8,6]{1,2,0:T(8,128)S(1)}, s32[8,8,6]{1,2,0:T(8,128)}, u32[]{:S(2)}) copy-start(s32[8,8,6]{1,2,0:T(8,128)} %copy.243) | copy-start | bytes 4612
  581.8 15.7 %copy-start.9 = (pred[8,8,6]{1,2,0:T(8,128)(4,1)S(1)}, pred[8,8,6]{1,2,0:T(8,128)(4,1)}, u32[]{:S(2)}) copy-start(pred[8,8,6]{1,2,0:T(8,128)(4,1)} %copy.247) | copy-start | bytes 1156
  597.5 15.6 %copy-start.5 = (s32[8,8,6]{1,2,0:T(8,128)S(1)}, s32[8,8,6]{1,2,0:T(8,128)}, u32[]{:S(2)}) copy-start(s32[8,8,6]{1,2,0:T(8,128)} %copy.254) | copy-start | bytes 4612
  613.1 15.9 %copy-start.6 = (s32[8,8,6]{1,2,0:T(8,128)S(1)}, s32[8,8,6]{1,2,0:T(8,128)}, u32[]{:S(2)}) copy-start(s32[8,8,6]{1,2,0:T(8,128)} %copy.265) | copy-start | bytes 4612
  613.1 15.9 %copy-start.11 = (pred[8,8,6]{1,2,0:T(8,128)(4,1)S(1)}, pred[8,8,6]{1,2,0:T(8,128)(4,1)}, u32[]{:S(2)}) copy-start(pred[8,8,6]{1,2,0:T(8,128)(4,1)} %copy.269) | copy-start | bytes 1156
  629.0 19.4 %copy-start.12 = (s32[8,1,8]{2,1,0:T(1,128)S(1)}, s32[8,1,8]{2,1,0:T(1,128)}, u32[]{:S(2)}) copy-start(s32[8,1,8]{2,1,0:T(1,128)} %param.23) | copy-start | bytes 772
  629.0 19.7 %copy-start.18 = (s32[8]{0:T(128)S(1)}, s32[8]{0:T(128)}, u32[]{:S(2)}) copy-start(s32[8]{0:T(128)} %copy-done.17) | copy-start | bytes 100
  629.0 48.3 %copy-start.1 = (bf16[1,32,2,128,128]{4,3,2,1,0:T(8,128)(2,1)S(1)}, bf16[1,32,2,128,128]{4,3,2,1,0:T(8,128)(2,1)}, u32[]{:S(2)}) copy-start(bf16[1,32,2,128,128]{4,3,2,1,0:T(8,128)(2,1)} %param.15) | copy-start | bytes 6291460
  (2 other events, 24.1 us)
Sparse Core Ops, SparseCore 0:
  9.3 283.7 all-gather.1
  648.6 21.1 all-reduce.1
where the time goes:
time: 692 us; the launch traced here: 684 us
  local copies, waits for them, and re-layouts  259 us (37%)
  waiting for transfers between devices  228 us (33%)
  matrix products  120 us (17%)
  starting transfers between devices  35.6 us (5%)
  blocking collectives  18.1 us (3%)
  between operations  14.6 us (2%)
  other arithmetic  7.82 us (1%)
    gather x8, local copies, waits for them, and re-layouts, on_device(): selected_entries = jnp.take(layer_blocks, layer_row_index, axis=0)  135 us
    transpose x4, local copies, waits for them, and re-layouts, on_device(): jnp.einsum('rvab,rvsbe->rvsae', block_tiles, selected_entries, preferred_...  99.4 us
    all_gather x1, waiting for transfers between devices, on_device(): lax.all_gather(b_blocks, 'row', axis=0, tiled=True)  95.8 us
    dot_general x4, matrix products, on_device(): jnp.einsum('ruvs,rvsae->ruae', mapping, block_products, precision=lax.Pre...  66.5 us
    dot_general x4, matrix products, on_device(): jnp.einsum('rvab,rvsbe->rvsae', block_tiles, selected_entries, preferred_...  53.9 us
    ppermute x9, waiting for transfers between devices, shifted(): lax.ppermute(value, axis, [(i, (i + by) % length) for i in range(length)])  45.5 us
    all_to_all x1, waiting for transfers between devices, on_device(): lax.all_to_all(outgoing_live_flags.reshape((pair_count,) + lead_shape[2:]...  37.3 us
    all_to_all x1, waiting for transfers between devices, on_device(): lax.all_to_all(send_blocks.reshape((pair_count,) + lead_shape[2:] + (bloc...  27.6 us
  transfers between devices with their start and end apart: 15, of which 8 were waited for; matrix products, arithmetic and copies ran while one was open for 40% of the time, Pallas kernels for 0%

commit v1 on v0

--- a/solution.py
+++ b/solution.py
@@ -4,6 +4,18 @@
 from jax.sharding import PartitionSpec as P
 
 GW = 10
+
+
+def gather_by_bits(shard, axis, dim):
+    ways, here, turn = (lax.axis_size(axis), lax.axis_index(axis), shard.shape[dim])
+    line, have = (shard, 1)
+    while have < ways:
+        line = jnp.concatenate(
+            [line, lax.ppermute(line, axis, [(d, (d - have) % ways) for d in range(ways)])],
+            axis=dim,
+        )
+        have = 2 * have
+    return jnp.roll(line, here * turn, axis=dim)
 
 
 def shifted(value, axis, by):
@@ -81,7 +93,7 @@
     columns = got_columns.reshape(panel_count, -1)
     live_flags = got_live.reshape(panel_count, -1)
     layer_blocks, layer_columns, layer_active_flags = (
-        lax.all_gather(b_blocks, "row", axis=0, tiled=True),
+        gather_by_bits(b_blocks, "row", 0),
         lax.all_gather(b_columns, "row", axis=0, tiled=True),
         lax.all_gather(b_live, "row", axis=0, tiled=True),
     )

time: 692 us -> 1150 us (1.66)
  blocking collectives: 18.1 us -> 330 us
  local copies, waits for them, and re-layouts: 259 us -> 347 us
  waiting for transfers between devices: 228 us -> 270 us
    all_gather x1, blocking collectives: 9.06 us -> 322 us  [on_device(): lax.all_gather(b_columns, 'row', axis=0, tiled=True)]
    ppermute x0 -> x2, waiting for transfers between devices: none -> 169 us  [gather_by_bits(): lax.ppermute(line, axis, [(d, (d - have) % ways) for d in range(ways)])]
    all_gather x1 -> x0, waiting for transfers between devices: 95.8 us -> none  [on_device(): lax.all_gather(b_blocks, 'row', axis=0, tiled=True)]
    unnamed x41 -> x52, local copies, waits for them, and re-layouts: 0.34 us -> 53.7 us
    all_to_all x1, waiting for transfers between devices: 27.6 us -> 0.01 us  [on_device(): lax.all_to_all(send_blocks.reshape((pair_count,) + lead_shape[2:] + (bloc...]
    reshape x0 -> x1, local copies, waits for them, and re-layouts: none -> 21.8 us  [on_device(): layer_blocks = layer_blocks.reshape(-1, list_width, block_edge, block_edge)]
    concatenate x0 -> x1, local copies, waits for them, and re-layouts: none -> 13.5 us  [gather_by_bits(): return jnp.roll(line, here * turn, axis=dim)]
    concatenate x0 -> x1, other arithmetic: none -> 11.9 us  [gather_by_bits(): jnp.concatenate([line, lax.ppermute(line, axis, [(d, (d - have) % ways) f...]
  transfers between devices with their start and end apart: 15 -> 16, of which waited for: 8 -> 7; matrix products, arithmetic and copies ran while one was open for 40% -> 32% of each run, Pallas kernels for 0% -> 0%
where the time goes in v1:
time: 1150 us; the launch traced here: 1140 us
  local copies, waits for them, and re-layouts  347 us (30%)
  blocking collectives  330 us (29%)
  waiting for transfers between devices  270 us (23%)
  matrix products  121 us (11%)
  starting transfers between devices  40.9 us (4%)
  other arithmetic  18.9 us (2%)
  between operations  14.5 us (1%)
    all_gather x1, blocking collectives, on_device(): lax.all_gather(b_columns, 'row', axis=0, tiled=True)  322 us
    ppermute x2, waiting for transfers between devices, gather_by_bits(): lax.ppermute(line, axis, [(d, (d - have) % ways) for d in range(ways)])  169 us
    gather x8, local copies, waits for them, and re-layouts, on_device(): selected_entries = jnp.take(layer_blocks, layer_row_index, axis=0)  135 us
    transpose x4, local copies, waits for them, and re-layouts, on_device(): jnp.einsum('rvab,rvsbe->rvsae', block_tiles, selected_entries, preferred_...  99.2 us
    dot_general x4, matrix products, on_device(): jnp.einsum('ruvs,rvsae->ruae', mapping, block_products, precision=lax.Pre...  66.8 us
    dot_general x4, matrix products, on_device(): jnp.einsum('rvab,rvsbe->rvsae', block_tiles, selected_entries, preferred_...  54.6 us
    unnamed x52, local copies, waits for them, and re-layouts  53.7 us
    ppermute x9, waiting for transfers between devices, shifted(): lax.ppermute(value, axis, [(i, (i + by) % length) for i in range(length)])  44.4 us
  transfers between devices with their start and end apart: 16, of which 7 were waited for; matrix products, arithmetic and copies ran while one was open for 32% of the time, Pallas kernels for 0%

profile of v1, /device:TPU:0, one launch (start us, length us, event | category | flops | bytes accessed | tf_op | source)
XLA Modules:
  0.0 1143.0 jit_solution(3638023576839842180)
XLA Ops:
  10.4 168.8 %collective-permute-done = bf16[40,1,6,128,128]{4,3,2,1,0:T(8,128)(2,1)S(1)} collective-permute-done((bf16[40,1,6,128,128]{4,3,2,1,0:T(8,128)(2,1)}, bf16[40,1,6,128,128]{4,3,2,1,0:T(8,128)(2,1)S(1)}, u32[]{:S(2)}, u32[]{:S(2)}) %collective-permute-start) | collective-permute-done | bytes 7864352 | tf_op jit(solution)/shard_map/ppermute | solution.py:14
  179.2 11.9 %pad_maximum_fusion = bf16[80,1,6,128,128]{4,3,2,1,0:T(8,128)(2,1)} fusion(bf16[40,1,6,128,128]{4,3,2,1,0:T(8,128)(2,1)S(1)} %collective-permute-done, bf16[40,1,6,128,128]{4,3,2,1,0:T(8,128)(2,1)} %param.19), kind=kLoop, calls=%fused_computation.18 | loop fusion | flops 7864320 | bytes 31457280 | tf_op jit(solution)/shard_map/concatenate | solution.py:13
  212.6 321.8 %all_gather.6 = s32[160,1,6]{2,0,1:T(8,128)S(1)} all-gather(s32[40,1,6]{2,0,1:T(8,128)S(1)} %copy.221), channel_id=1, replica_groups=mesh['row'=4,'col'=4,'depth'=2] {'row'}, dimensions={0}, use_global_device_ids=true | all-gather | bytes 4800 | tf_op jit(solution)/shard_map/all_gather | solution.py:97
  571.9 37.0 %all-to-all-done.2 = s32[8,1,4,2]{2,3,1,0:T(2,128)S(1)} async-done(((s32[8,1,4,2]{2,3,1,0:T(2,128)}), s32[8,1,4,2]{2,3,1,0:T(2,128)S(1)}, u32[]{:S(2)}, u32[]{:S(2)}) %all-to-all-start.2) | async-done | bytes 288 | tf_op jit(solution)/shard_map/all_to_all | solution.py:71
  622.1 42.8 %collective-permute-done.6 = s32[8,8]{0,1:T(8,128)S(1)} collective-permute-done((s32[8,8]{0,1:T(8,128)S(1)}, s32[8,8]{0,1:T(8,128)S(1)}, u32[]{:S(2)}, u32[]{:S(2)}) %collective-permute-start.6) | collective-permute-done | bytes 288 | tf_op jit(solution)/shard_map/ppermute | solution.py:23
  675.9 9.8 constant_dynamic-update-slice_fusion.4
  685.6 13.7 %constant_dynamic-update-slice_fusion.3 = bf16[320,1,6,128,128]{4,3,2,1,0:T(8,128)(2,1)} fusion(bf16[320,1,6,128,128]{4,3,2,1,0:T(8,128)(2,1)} %constant_dynamic-update-slice_fusion.4, bf16[80,1,6,128,128]{4,3,2,1,0:T(8,128)(2,1)} %collective-permute-done.1), kind=kLoop, calls=%fused_computation.97 | loop fusion | bytes 31457280
  699.4 9.8 constant_dynamic-update-slice_fusion.2
  709.2 9.8 constant_dynamic-update-slice_fusion.1
  719.0 13.5 %constant_dynamic-update-slice_fusion = bf16[320,1,6,128,128]{4,3,2,1,0:T(8,128)(2,1)} fusion(bf16[320,1,6,128,128]{4,3,2,1,0:T(8,128)(2,1)} %constant_dynamic-update-slice_fusion.1, bf16[80,1,6,128,128]{4,3,2,1,0:T(8,128)(2,1)} %collective-permute-done.1), kind=kLoop, calls=%fused_computation.94 | loop fusion | bytes 31457280 | tf_op jit(solution)/shard_map/jit(_roll_dynamic)/concatenate | solution.py:18
  732.5 21.8 %dynamic-slice_bitcast_fusion = bf16[160,6,128,128]{3,2,1,0:T(8,128)(2,1)} fusion(bf16[320,1,6,128,128]{4,3,2,1,0:T(8,128)(2,1)} %constant_dynamic-update-slice_fusion, s32[]{:T(128)S(6)} %select_n.229), kind=kLoop, calls=%fused_computation.17 | loop fusion | bytes 62914564 | tf_op jit(solution)/shard_map/reshape | solution.py:101
  754.3 17.2 %gather_fusion.13 = bf16[64,6,128,128]{3,2,1,0:T(8,128)(2,1)} fusion(bf16[160,6,128,128]{3,2,1,0:T(8,128)(2,1)} %dynamic-slice_bitcast_fusion, s32[1024]{0:T(1024)S(1)} %pad_clamp_fusion.2), kind=kCustom, calls=%fused_computation.12.clone | custom fusion | bytes 25166080 | tf_op jit(solution)/shard_map/jit(_take)/gather | solution.py:113
  771.5 17.2 %gather_fusion.10 = bf16[64,6,128,128]{3,2,1,0:T(8,128)(2,1)} fusion(bf16[160,6,128,128]{3,2,1,0:T(8,128)(2,1)} %dynamic-slice_bitcast_fusion, s32[1024]{0:T(1024)S(1)} %pad_clamp_fusion.3), kind=kCustom, calls=%fused_computation.11.clone | custom fusion | bytes 25166080 | tf_op jit(solution)/shard_map/jit(_take)/gather | solution.py:113
  788.7 15.9 %copy.257 = bf16[8,8,6,128,128]{3,4,2,1,0:T(8,128)(2,1)} copy(bf16[8,8,6,128,128]{4,3,2,1,0:T(8,128)(2,1)} %bitcast.150) | data formatting | bytes 25165824 | tf_op jit(solution)/shard_map/jit(_take)/gather | solution.py:113
  804.5 16.6 %copy.246 = bf16[8,8,6,128,128]{3,4,2,1,0:T(8,128)(2,1)} copy(bf16[8,8,6,128,128]{4,3,2,1,0:T(8,128)(2,1)} %bitcast.151) | data formatting | bytes 25165824 | tf_op jit(solution)/shard_map/jit(_take)/gather | solution.py:113
  821.2 13.6 %fusion.18 = f32[8,8,6,128,128]{3,4,2,1,0:T(8,128)} fusion(bf16[8,8,6,128,128]{3,4,2,1,0:T(8,128)(2,1)} %copy.257, pred[8,8]{1,0:T(8,128)(4,1)S(1)} %copy.248, bf16[8,8,128,128]{3,2,1,0:T(8,128)(2,1)} %collective-permute-done.7), kind=kOutput, calls=%fused_computation.33 | convolution fusion | flops 1616904192 | bytes 39845952 | tf_op jit(solution)/shard_map/rvab,rvsbe->rvsae/dot_general | solution.py:114
  834.8 13.7 %fusion.15 = f32[8,8,6,128,128]{3,4,2,1,0:T(8,128)} fusion(bf16[8,8,6,128,128]{3,4,2,1,0:T(8,128)(2,1)} %copy.246, pred[8,8]{1,0:T(8,128)(4,1)S(1)} %copy.237, bf16[8,8,128,128]{3,2,1,0:T(8,128)(2,1)} %collective-permute-done.4), kind=kOutput, calls=%fused_computation.32 | convolution fusion | flops 1616904192 | bytes 39845952 | tf_op jit(solution)/shard_map/rvab,rvsbe->rvsae/dot_general | solution.py:114
  848.5 17.4 %gather_fusion.7 = bf16[64,6,128,128]{3,2,1,0:T(8,128)(2,1)} fusion(bf16[160,6,128,128]{3,2,1,0:T(8,128)(2,1)} %dynamic-slice_bitcast_fusion, s32[1024]{0:T(1024)S(1)} %pad_clamp_fusion.6), kind=kCustom, calls=%fused_computation.2.clone | custom fusion | bytes 25166080 | tf_op jit(solution)/shard_map/jit(_take)/gather | solution.py:113
  865.9 17.2 %gather_fusion.16 = bf16[64,6,128,128]{3,2,1,0:T(8,128)(2,1)} fusion(bf16[160,6,128,128]{3,2,1,0:T(8,128)(2,1)} %dynamic-slice_bitcast_fusion, s32[1024]{0:T(1024)S(1)} %pad_clamp_fusion.1), kind=kCustom, calls=%fused_computation.13.clone | custom fusion | bytes 25166080 | tf_op jit(solution)/shard_map/jit(_take)/gather | solution.py:113
  883.1 24.8 %copy.258 = f32[8,8,6,128,128]{4,1,2,3,0:T(8,128)} copy(f32[8,8,6,128,128]{3,4,2,1,0:T(8,128)} %fusion.18) | data formatting | bytes 50331648 | tf_op jit(solution)/shard_map/rvab,rvsbe->rvsae/transpose | solution.py:114
  907.9 24.8 %copy.247 = f32[8,8,6,128,128]{4,1,2,3,0:T(8,128)} copy(f32[8,8,6,128,128]{3,4,2,1,0:T(8,128)} %fusion.15) | data formatting | bytes 50331648 | tf_op jit(solution)/shard_map/rvab,rvsbe->rvsae/transpose | solution.py:114
  932.7 16.6 %copy.235 = bf16[8,8,6,128,128]{3,4,2,1,0:T(8,128)(2,1)} copy(bf16[8,8,6,128,128]{4,3,2,1,0:T(8,128)(2,1)} %bitcast.149) | data formatting | bytes 25165824 | tf_op jit(solution)/shard_map/jit(_take)/gather | solution.py:113
  949.3 13.7 %fusion.12 = f32[8,8,6,128,128]{3,4,2,1,0:T(8,128)} fusion(bf16[8,8,128,128,1]{3,2,4,1,0:T(8,128)(2,1)} %bitcast.24, bf16[8,8,6,128,128]{3,4,2,1,0:T(8,128)(2,1)} %copy.235, pred[8,8]{1,0:T(8,128)(4,1)S(1)} %copy.220), kind=kOutput, calls=%fused_computation.31 | convolution fusion | flops 1616904192 | bytes 39845952 | tf_op jit(solution)/shard_map/rvab,rvsbe->rvsae/dot_general | solution.py:114
  963.0 24.8 %copy.236 = f32[8,8,6,128,128]{4,1,2,3,0:T(8,128)} copy(f32[8,8,6,128,128]{3,4,2,1,0:T(8,128)} %fusion.12) | data formatting | bytes 50331648 | tf_op jit(solution)/shard_map/rvab,rvsbe->rvsae/transpose | solution.py:114
  987.8 16.7 %copy.268 = bf16[8,8,6,128,128]{3,4,2,1,0:T(8,128)(2,1)} copy(bf16[8,8,6,128,128]{4,3,2,1,0:T(8,128)(2,1)} %bitcast.148) | data formatting | bytes 25165824 | tf_op jit(solution)/shard_map/jit(_take)/gather | solution.py:113
  1004.4 13.7 %fusion.21 = f32[8,8,6,128,128]{3,4,2,1,0:T(8,128)} fusion(bf16[8,8,6,128,128]{3,4,2,1,0:T(8,128)(2,1)} %copy.268, pred[8,8]{1,0:T(8,128)(4,1)S(1)} %copy-done.10, bf16[8,8,128,128]{3,2,1,0:T(8,128)(2,1)} %collective-permute-done.10), kind=kOutput, calls=%fused_computation.34 | convolution fusion | flops 1616904192 | bytes 39845952 | tf_op jit(solution)/shard_map/rvab,rvsbe->rvsae/dot_general | solution.py:114
  1018.1 24.8 %copy.269 = f32[8,8,6,128,128]{4,1,2,3,0:T(8,128)} copy(f32[8,8,6,128,128]{3,4,2,1,0:T(8,128)} %fusion.21) | data formatting | bytes 50331648 | tf_op jit(solution)/shard_map/rvab,rvsbe->rvsae/transpose | solution.py:114
  1042.9 16.0 %fusion.35 = f32[8,8,128,128,1]{3,1,4,2,0:T(8,128)} fusion(f32[8,8,6,128,128]{4,1,2,3,0:T(8,128)} %copy.258, s32[8,8,6]{1,2,0:T(8,128)S(1)} %copy-done.6, s32[8,8]{1,0:T(8,128)S(1)} %copy-done.8, pred[8,8,6]{1,2,0:T(8,128)(4,1)S(1)} %copy-done.13), kind=kOutput, calls=%fused_computation.52 | convolution fusion | flops 603985920 | bytes 29362304 | tf_op jit(solution)/shard_map/ruvs,rvsae->ruae/dot_general | solution.py:117
  1058.9 15.6 %fusion.37 = f32[8,8,128,128,1]{3,1,4,2,0:T(8,128)} fusion(f32[8,8,6,128,128]{4,1,2,3,0:T(8,128)} %copy.247, s32[8,8,6]{1,2,0:T(8,128)S(1)} %copy-done.5, s32[8,8]{1,0:T(8,128)S(1)} %copy-done.8, pred[8,8,6]{1,2,0:T(8,128)(4,1)S(1)} %copy-done.12), kind=kOutput, calls=%fused_computation.54 | convolution fusion | flops 603985920 | bytes 29362304 | tf_op jit(solution)/shard_map/ruvs,rvsae->ruae/dot_general | solution.py:117
  1074.6 15.6 %fusion.39 = f32[8,8,128,128,1]{3,1,4,2,0:T(8,128)} fusion(f32[8,8,6,128,128]{4,1,2,3,0:T(8,128)} %copy.236, s32[8,8]{1,0:T(8,128)S(1)} %copy-done.8, s32[8,8,6]{1,2,0:T(8,128)S(1)} %copy-done.4, pred[8,8,6]{1,2,0:T(8,128)(4,1)S(1)} %copy-done.11), kind=kOutput, calls=%fused_computation.56 | convolution fusion | flops 603985920 | bytes 29362304 | tf_op jit(solution)/shard_map/ruvs,rvsae->ruae/dot_general | solution.py:117
  1090.2 19.6 %fusion.28 = bf16[8,8,128,128]{3,1,2,0:T(8,128)(2,1)} fusion(f32[8,8,128,128,1]{3,1,4,2,0:T(8,128)} %fusion.35, f32[8,8,128,128,1]{3,1,4,2,0:T(8,128)} %fusion.37, f32[8,8,128,128,1]{3,1,4,2,0:T(8,128)} %fusion.39, f32[8,8,6,128,128]{4,1,2,3,0:T(8,128)} %copy.269, s32[8,8,6]{1,2,0:T(8,128)S(1)} %copy-done.7, s32[8,8]{1,0:T(8,128)S(1)} %copy-done.8, ...), kind=kOutput, calls=%fused_computation.40 | convolution fusion | flops 608180224 | bytes 39848064 | tf_op jit(solution)/shard_map/ruvs,rvsae->ruae/dot_general | solution.py:117
  1110.2 18.2 %all-reduce.2.cloned.1.call-done = bf16[8,8,128,128]{3,1,2,0:T(8,128)(2,1)} async-done(((bf16[8,8,128,128]{3,1,2,0:T(8,128)(2,1)}), bf16[8,8,128,128]{3,1,2,0:T(8,128)(2,1)}) %all-reduce.2.cloned.1.call-update) | async-done | bytes 2097168 | tf_op jit(solution)/shard_map/psum | solution.py:126
  (175 shorter events, 94.3 us)
Async XLA Ops:
  6.5 192.5 %copy-start = (bf16[1,32,2,128,128]{4,3,2,1,0:T(8,128)(2,1)S(1)}, bf16[1,32,2,128,128]{4,3,2,1,0:T(8,128)(2,1)}, u32[]{:S(2)}) copy-start(bf16[1,32,2,128,128]{4,3,2,1,0:T(8,128)(2,1)} %param.15) | copy-start | bytes 6291460
  6.5 172.7 %collective-permute-start = (bf16[40,1,6,128,128]{4,3,2,1,0:T(8,128)(2,1)}, bf16[40,1,6,128,128]{4,3,2,1,0:T(8,128)(2,1)S(1)}, u32[]{:S(2)}, u32[]{:S(2)}) collective-permute-start(bf16[40,1,6,128,128]{4,3,2,1,0:T(8,128)(2,1)} %param.19), channel_id=1, source_target_pairs={{0,24},{8,0},{16,8},{24,16},{1,25},{9,1},{17,9},{25,17},{2,26},{10... | collective-permute-start | bytes 23592968 | tf_op jit(solution)/shard_map/ppermute | solution.py:14
  191.1 18.4 %copy-start.18 = (s32[1,32,2]{1,2,0:T(2,128)S(1)}, s32[1,32,2]{1,2,0:T(2,128)}, u32[]{:S(2)}) copy-start(s32[1,32,2]{1,2,0:T(2,128)} %param.17) | copy-start | bytes 772
  191.1 19.2 %copy-start.19 = (s32[1,32,2]{1,2,0:T(2,128)S(1)}, s32[1,32,2]{1,2,0:T(2,128)}, u32[]{:S(2)}) copy-start(s32[1,32,2]{1,2,0:T(2,128)} %param.16) | copy-start | bytes 772
  191.1 20.6 %copy-start.16 = (s32[40,1,6]{0,1,2:T(1,128)S(1)}, s32[40,1,6]{0,1,2:T(1,128)}, u32[]{:S(2)}) copy-start(s32[40,1,6]{0,1,2:T(1,128)} %param.20) | copy-start | bytes 2884
  191.1 20.7 %copy-start.17 = (s32[40,1,6]{0,1,2:T(1,128)S(1)}, s32[40,1,6]{0,1,2:T(1,128)}, u32[]{:S(2)}) copy-start(s32[40,1,6]{0,1,2:T(1,128)} %param.21) | copy-start | bytes 2884
  191.1 494.5 %collective-permute-start.1 = (bf16[80,1,6,128,128]{4,3,2,1,0:T(8,128)(2,1)}, bf16[80,1,6,128,128]{4,3,2,1,0:T(8,128)(2,1)}, u32[]{:S(2)}, u32[]{:S(2)}) collective-permute-start(bf16[80,1,6,128,128]{4,3,2,1,0:T(8,128)(2,1)} %pad_maximum_fusion), channel_id=1, source_target_pairs={{0,16},{8,24},{16,0},{24,8},{1,17},{9,25},{17,1},{25,9},{2,18},{10... | collective-permute-start | bytes 47185928 | tf_op jit(solution)/shard_map/ppermute | solution.py:14
  193.9 10.5 all-to-all-start
  201.2 361.0 %copy-start.3 = (s32[8,1,8]{2,1,0:T(1,128)S(1)}, s32[8,1,8]{2,1,0:T(1,128)}, u32[]{:S(2)}) copy-start(s32[8,1,8]{2,1,0:T(1,128)} %param.22) | copy-start | bytes 772
  204.4 348.6 %all-to-all-start.3 = ((bf16[8,1,4,2,128,128]{5,4,3,2,1,0:T(8,128)(2,1)}), bf16[8,1,4,2,128,128]{5,4,3,2,1,0:T(8,128)(2,1)}, u32[]{:S(2)}, u32[]{:S(2)}) async-start(bf16[8,1,4,2,128,128]{5,4,3,2,1,0:T(8,128)(2,1)} %broadcast_select_fusion), calls=%async_computation.3 | async-start | bytes 4194304 | tf_op jit(solution)/shard_map/all_to_all | solution.py:57
  553.5 10.5 all-to-all-start.1
  558.4 59.5 %collective-permute-start.4 = (bf16[8,8,128,128]{3,2,1,0:T(8,128)(2,1)}, bf16[8,8,128,128]{3,2,1,0:T(8,128)(2,1)}, u32[]{:S(2)}, u32[]{:S(2)}) collective-permute-start(bf16[8,8,128,128]{3,2,1,0:T(8,128)(2,1)} %bitcast.22), channel_id=1, source_target_pairs={{0,6},{2,0},{4,2},{6,4},{1,7},{3,1},{5,3},{7,5},{8,14},{10,8},{12,... | collective-permute-start | bytes 6291464 | tf_op jit(solution)/shard_map/ppermute | solution.py:23
  564.0 44.8 %all-to-all-start.2 = ((s32[8,1,4,2]{2,3,1,0:T(2,128)}), s32[8,1,4,2]{2,3,1,0:T(2,128)S(1)}, u32[]{:S(2)}, u32[]{:S(2)}) async-start(s32[8,1,4,2]{2,3,1,0:T(2,128)} %copy.229), calls=%async_computation.2 | async-start | bytes 16384 | tf_op jit(solution)/shard_map/all_to_all | solution.py:71
  567.4 561.0 %all-reduce.2.cloned.1.call-start = ((), (), s32[]{:S(2)}) async-start(), calls=%async_computation.4 | async-start | bytes 4194304 | tf_op jit(solution)/shard_map/psum | solution.py:126
  568.2 47.3 %collective-permute-start.2 = (s32[8,8]{0,1:T(8,128)S(1)}, s32[8,8]{0,1:T(8,128)S(1)}, u32[]{:S(2)}, u32[]{:S(2)}) collective-permute-start(s32[8,8]{0,1:T(8,128)S(1)} %bitcast.164), channel_id=1, source_target_pairs={{0,6},{2,0},{4,2},{6,4},{1,7},{3,1},{5,3},{7,5},{8,14},{10,8},{12,... | collective-permute-start | bytes 776 | tf_op jit(solution)/shard_map/ppermute | solution.py:23
  609.0 8.0 collective-permute-start.3
  617.0 3.6 collective-permute-start.5
  617.9 55.5 %collective-permute-start.7 = (bf16[8,8,128,128]{3,2,1,0:T(8,128)(2,1)}, bf16[8,8,128,128]{3,2,1,0:T(8,128)(2,1)}, u32[]{:S(2)}, u32[]{:S(2)}) collective-permute-start(bf16[8,8,128,128]{3,2,1,0:T(8,128)(2,1)} %collective-permute-done.4), channel_id=1, source_target_pairs={{0,6},{2,0},{4,2},{6,4},{1,7},{3,1},{5,3},{7,5},{8,14},{10,8},{12,... | collective-permute-start | bytes 6291464 | tf_op jit(solution)/shard_map/ppermute | solution.py:23
  619.7 45.2 %collective-permute-start.6 = (s32[8,8]{0,1:T(8,128)S(1)}, s32[8,8]{0,1:T(8,128)S(1)}, u32[]{:S(2)}, u32[]{:S(2)}) collective-permute-start(s32[8,8]{0,1:T(8,128)S(1)} %collective-permute-done.3), channel_id=1, source_target_pairs={{0,6},{2,0},{4,2},{6,4},{1,7},{3,1},{5,3},{7,5},{8,14},{10,8},{12,... | collective-permute-start | bytes 776 | tf_op jit(solution)/shard_map/ppermute | solution.py:23
  665.0 3.9 collective-permute-start.8
  668.9 3.6 collective-permute-start.9
  669.2 30.2 %copy-start.9 = (pred[8,8]{1,0:T(8,128)(4,1)}, pred[8,8]{1,0:T(8,128)(4,1)S(1)}, u32[]{:S(2)}) copy-start(pred[8,8]{1,0:T(8,128)(4,1)S(1)} %copy.259) | copy-start | bytes 196
  673.4 331.0 %collective-permute-start.10 = (bf16[8,8,128,128]{3,2,1,0:T(8,128)(2,1)}, bf16[8,8,128,128]{3,2,1,0:T(8,128)(2,1)}, u32[]{:S(2)}, u32[]{:S(2)}) collective-permute-start(bf16[8,8,128,128]{3,2,1,0:T(8,128)(2,1)} %collective-permute-done.7), channel_id=1, source_target_pairs={{0,6},{2,0},{4,2},{6,4},{1,7},{3,1},{5,3},{7,5},{8,14},{10,8},{12,... | collective-permute-start | bytes 6291464 | tf_op jit(solution)/shard_map/ppermute | solution.py:23
  987.8 16.7 %copy-start.10 = (pred[8,8]{1,0:T(8,128)(4,1)S(1)}, pred[8,8]{1,0:T(8,128)(4,1)}, u32[]{:S(2)}) copy-start(pred[8,8]{1,0:T(8,128)(4,1)} %copy-done.9) | copy-start | bytes 196
  1018.1 24.8 %copy-start.6 = (s32[8,8,6]{1,2,0:T(8,128)S(1)}, s32[8,8,6]{1,2,0:T(8,128)}, u32[]{:S(2)}) copy-start(s32[8,8,6]{1,2,0:T(8,128)} %copy.250) | copy-start | bytes 4612
  1018.1 24.8 %copy-start.8 = (s32[8,8]{1,0:T(8,128)S(1)}, s32[8,8]{1,0:T(8,128)}, u32[]{:S(2)}) copy-start(s32[8,8]{1,0:T(8,128)} %broadcast_select_fusion.1) | copy-start | bytes 772
  1018.1 24.8 %copy-start.13 = (pred[8,8,6]{1,2,0:T(8,128)(4,1)S(1)}, pred[8,8,6]{1,2,0:T(8,128)(4,1)}, u32[]{:S(2)}) copy-start(pred[8,8,6]{1,2,0:T(8,128)(4,1)} %copy.254) | copy-start | bytes 1156
  1042.9 16.0 %copy-start.5 = (s32[8,8,6]{1,2,0:T(8,128)S(1)}, s32[8,8,6]{1,2,0:T(8,128)}, u32[]{:S(2)}) copy-start(s32[8,8,6]{1,2,0:T(8,128)} %copy.239) | copy-start | bytes 4612
  1042.9 16.0 %copy-start.12 = (pred[8,8,6]{1,2,0:T(8,128)(4,1)S(1)}, pred[8,8,6]{1,2,0:T(8,128)(4,1)}, u32[]{:S(2)}) copy-start(pred[8,8,6]{1,2,0:T(8,128)(4,1)} %copy.243) | copy-start | bytes 1156
  1090.2 19.7 %copy-start.15 = (s32[8,1,8]{2,1,0:T(1,128)S(1)}, s32[8,1,8]{2,1,0:T(1,128)}, u32[]{:S(2)}) copy-start(s32[8,1,8]{2,1,0:T(1,128)} %param.23) | copy-start | bytes 772
  1090.2 19.9 %copy-start.21 = (s32[8]{0:T(128)S(1)}, s32[8]{0:T(128)}, u32[]{:S(2)}) copy-start(s32[8]{0:T(128)} %copy-done.20) | copy-start | bytes 100
  1090.2 45.8 %copy-start.1 = (bf16[1,32,2,128,128]{4,3,2,1,0:T(8,128)(2,1)S(1)}, bf16[1,32,2,128,128]{4,3,2,1,0:T(8,128)(2,1)}, u32[]{:S(2)}) copy-start(bf16[1,32,2,128,128]{4,3,2,1,0:T(8,128)(2,1)} %param.15) | copy-start | bytes 6291460
  (6 other events, 74.9 us)
Sparse Core Ops, SparseCore 0:
  1109.9 18.4 all-reduce.1
